TPU v7x, 256 devices: a whole 4x4x8 slice. The times are simulated.
256 devices in a mesh: tile: 4 (over x), expert: 64 (over y, z, core).
Axes of the slice: x: 4, y: 4, z: 8, core: 2. Of those that a mesh axis runs over, the one named last changes fastest.
Arguments:
- patches: bfloat16 [64, 16, 32, 1152], P('expert', 'tile'), may hold values from -6 to 6
- norm1_gain: float32 [1152], replicated, may hold values from 0.1 to 1.9
- qkv_weight: bfloat16 [1152, 3, 1152], P(None, None, 'tile'), may hold values from -8 to 8
- qkv_bias: float32 [3, 1152], P(None, 'tile'), may hold values from -3 to 3
- out_weight: bfloat16 [1152, 1152], P('tile'), may hold values from -0.1875 to 0.1875
- out_bias: float32 [1152], replicated, may hold values from -3 to 3
- norm2_gain: float32 [1152], replicated, may hold values from 0.1 to 1.9
- proj_weight: bfloat16 [4608, 2048], P('expert', 'tile'), may hold values from -0.09375 to 0.09375
- moe_gain: float32 [2048], replicated, may hold values from 0.1 to 1.9
- expert_in: bfloat16 [64, 2048, 2, 1408], P('expert', None, None, 'tile'), may hold values from -0.125 to 0.125
- expert_out: bfloat16 [64, 1408, 2048], P('expert', 'tile'), may hold values from -0.15625 to 0.15625
- shared_in: bfloat16 [2048, 2, 1408], P(None, None, 'tile'), may hold values from -0.125 to 0.125
- shared_out: bfloat16 [1408, 2048], P('tile'), may hold values from -0.15625 to 0.15625
- routes: int32 [64, 8, 16, 6], P('expert'), may hold values from 0 to 63, all different within a row; in each aligned block of 32 rows (0 to 31, 32 to 63, ..., all dimensions but the last counted through in order) at most 6 rows name the same one
- gates: float32 [64, 8, 16, 6], P('expert', 'tile'), may hold values from 0.1 to 1
Outputs:
- moe_tokens: bfloat16 [64, 8, 16, 2048], P('expert', 'tile')
Inputs may be any that keep to these rules, and one draw needn't show every extreme that they name: `routes`: each merged token names 6 different experts. Flattening the merged tokens in the order page, row, column into aligned blocks of 32 (the merged tokens of one device), no expert is named more than 6 times in a block, a bound that some block reaches.
All inputs are finite; a program needn't handle non-finite values.
Results may differ from a plain program's by a relative error of at most 0.02.
Values may be sent and summed in bfloat16 or wider, within the bound.
A program may use at most 128 MiB of HBM per device.

v0:
```python
from functools import partial
import math

import jax
import jax.numpy as jnp
from jax import lax
from jax.sharding import PartitionSpec as P

HD = 72


norm_eps = 1e-06
rope_base = 10000.0


def layer_norm(values, gain_vec):
    centre = values - jnp.mean(values, axis=-1, keepdims=True)
    spread = jnp.mean(centre * centre, axis=-1, keepdims=True)
    return centre * lax.rsqrt(spread + norm_eps) * gain_vec


def rms_norm(values, gain_vec):
    return (
        values * lax.rsqrt(jnp.mean(values * values, axis=-1, keepdims=True) + norm_eps) * gain_vec
    )


def rope_tables(positions, columns, head_size):
    quarter = head_size // 4
    inverse = jnp.exp(jnp.arange(quarter).astype(jnp.float32) * (-math.log(rope_base) / quarter))
    row_angle = (positions // columns).astype(jnp.float32)[:, None] * inverse[None, :]
    col_angle = (positions % columns).astype(jnp.float32)[:, None] * inverse[None, :]
    return (jnp.cos(row_angle), jnp.sin(row_angle), jnp.cos(col_angle), jnp.sin(col_angle))


def rotate(values, tables):
    cos_row, sin_row, cos_col, sin_col = tables
    quarter = values.shape[-1] // 4
    row_a = values[..., :quarter]
    row_b = values[..., quarter : 2 * quarter]
    col_a = values[..., 2 * quarter : 3 * quarter]
    col_b = values[..., 3 * quarter :]
    return jnp.concatenate(
        [
            row_a * cos_row[:, None] - row_b * sin_row[:, None],
            row_b * cos_row[:, None] + row_a * sin_row[:, None],
            col_a * cos_col[:, None] - col_b * sin_col[:, None],
            col_b * cos_col[:, None] + col_a * sin_col[:, None],
        ],
        axis=-1,
    )


def attend(query_rows, key_rows, value_rows, divisor):
    count = query_rows.shape[0]
    width = min(count, 512)
    blocks = query_rows.reshape(count // width, width, query_rows.shape[1], query_rows.shape[2])

    def one_block(block):
        scores = (
            jnp.einsum("qhd,khd->hqk", block, key_rows, preferred_element_type=jnp.float32)
            / divisor
        )
        weights = jax.nn.softmax(scores, axis=-1).astype(jnp.bfloat16)
        return jnp.einsum(
            "hqk,khd->qhd", weights, value_rows, preferred_element_type=jnp.float32
        ).astype(jnp.bfloat16)

    return lax.map(one_block, blocks).reshape(count, -1)


def block_slots(block_routes, experts_count, capacity):
    picks = block_routes.reshape(-1)
    onehot = (picks[:, None] == jnp.arange(experts_count)[None, :]).astype(jnp.int32)
    earlier = jnp.cumsum(onehot, axis=0) - onehot
    ranks = jnp.sum(earlier * onehot, axis=1)
    owners_flat = jnp.arange(picks.shape[0]) // block_routes.shape[1]
    table = (
        jnp.full((experts_count * capacity,), -1, dtype=jnp.int32)
        .at[picks * capacity + ranks]
        .set(owners_flat)
    )
    return (ranks.reshape(block_routes.shape), table.reshape(experts_count, capacity))


def per_device(
    patches,
    norm1_gain,
    qkv_weight,
    qkv_bias,
    out_weight,
    out_bias,
    norm2_gain,
    proj_weight,
    moe_gain,
    expert_in,
    expert_out,
    shared_in,
    shared_out,
    routes,
    gates,
):
    tiles = lax.axis_size("tile")
    experts_count = lax.axis_size("expert")
    tile_id = lax.axis_index("tile")
    row_count = patches.shape[1]
    columns = patches.shape[2]
    width_vit = patches.shape[3]
    local_rows = row_count * columns
    inputs = patches.reshape(local_rows, width_vit).astype(jnp.float32)
    normed = layer_norm(inputs, norm1_gain).astype(jnp.bfloat16)
    heads_here = qkv_weight.shape[2] // HD
    qkv_flat = qkv_weight.reshape(width_vit, -1)
    bias_rows = qkv_bias.reshape(1, 3, heads_here, HD)
    piece = lax.all_gather(normed, "tile", axis=0, tiled=True)
    mixed = (
        jnp.dot(piece, qkv_flat, preferred_element_type=jnp.float32).reshape(
            piece.shape[0], 3, heads_here, HD
        )
        + bias_rows
    )
    tables = rope_tables(jnp.arange(piece.shape[0]), columns, HD)
    page_qkv = jnp.stack(
        [rotate(mixed[:, 0], tables), rotate(mixed[:, 1], tables), mixed[:, 2]], axis=1
    ).astype(jnp.bfloat16)
    attended = attend(page_qkv[:, 0], page_qkv[:, 1], page_qkv[:, 2], math.sqrt(HD))
    mixed_heads = lax.psum_scatter(
        jnp.dot(attended, out_weight, preferred_element_type=jnp.float32).astype(jnp.bfloat16),
        "tile",
        scatter_dimension=0,
        tiled=True,
    ).astype(jnp.float32)
    hidden = inputs + mixed_heads + out_bias
    normed_out = layer_norm(hidden, norm2_gain).astype(jnp.bfloat16)
    merged = (
        normed_out.reshape(row_count // 2, 2, columns // 2, 2, width_vit)
        .transpose(0, 2, 1, 3, 4)
        .reshape(-1, 4 * width_vit)
    )
    merged_count = merged.shape[0]
    group_merged = lax.all_gather(merged, "tile", axis=0, tiled=True)
    projected = jnp.dot(
        group_merged,
        lax.all_gather(proj_weight, "expert", axis=0, tiled=True),
        preferred_element_type=jnp.float32,
    ).astype(jnp.bfloat16)
    tokens_moe = lax.all_to_all(projected, "tile", split_axis=0, concat_axis=1, tiled=True)
    width_moe = tokens_moe.shape[1]
    moe_in = rms_norm(tokens_moe.astype(jnp.float32), moe_gain).astype(jnp.bfloat16)
    group_in = lax.all_gather(moe_in, "tile", axis=0, tiled=True)
    shared_gated = jnp.dot(
        group_in, shared_in.reshape(width_moe, -1), preferred_element_type=jnp.float32
    ).reshape(group_in.shape[0], 2, -1)
    shared_hidden = (jax.nn.silu(shared_gated[:, 0]) * shared_gated[:, 1]).astype(jnp.bfloat16)
    shared_part = lax.psum_scatter(
        jnp.dot(shared_hidden, shared_out, preferred_element_type=jnp.float32).astype(jnp.bfloat16),
        "tile",
        scatter_dimension=0,
        tiled=True,
    ).astype(jnp.float32)
    top_count = routes.shape[-1]
    capacity = max(2, min(merged_count, 2 * merged_count * top_count // experts_count))
    group_routes = routes.reshape(tiles, merged_count, top_count)
    group_ranks, group_owners = jax.vmap(
        partial(block_slots, experts_count=experts_count, capacity=capacity)
    )(group_routes)
    own_routes = lax.dynamic_index_in_dim(group_routes, tile_id, 0, keepdims=False)
    own_ranks = lax.dynamic_index_in_dim(group_ranks, tile_id, 0, keepdims=False)
    empty_value = jnp.zeros((), jnp.bfloat16)
    table = lax.dynamic_index_in_dim(group_owners, tile_id, 0, keepdims=False)
    used = table >= 0
    outgoing = jnp.where(used[..., None], moe_in[jnp.where(used, table, 0)], empty_value)
    received = lax.all_to_all(outgoing, "expert", split_axis=0, concat_axis=0, tiled=True)
    arrived = lax.all_gather(received[:, None], "tile", axis=1, tiled=True)
    slot_rows = arrived.reshape(-1, width_moe)
    gated = jnp.dot(
        slot_rows, expert_in.reshape(width_moe, -1), preferred_element_type=jnp.float32
    ).reshape(slot_rows.shape[0], 2, -1)
    expert_hidden = (jax.nn.silu(gated[:, 0]) * gated[:, 1]).astype(jnp.bfloat16)
    partial_out = (
        jnp.dot(
            expert_hidden,
            expert_out.reshape(expert_hidden.shape[1], width_moe),
            preferred_element_type=jnp.float32,
        )
        .astype(jnp.bfloat16)
        .reshape(arrived.shape)
    )
    came_back = lax.all_to_all(partial_out, "expert", split_axis=0, concat_axis=0, tiled=True)
    returned = lax.psum_scatter(
        came_back.astype(jnp.float32).astype(jnp.bfloat16), "tile", scatter_dimension=1, tiled=True
    )
    results_flat = returned.reshape(experts_count * capacity, width_moe)
    pick_index = own_routes * capacity + own_ranks
    gate_rows = gates.reshape(merged_count, top_count)
    routed = jnp.zeros((merged_count, width_moe), jnp.float32)
    for position in range(top_count):
        routed = routed + gate_rows[:, position : position + 1] * results_flat[
            pick_index[:, position]
        ].astype(jnp.float32)
    output = tokens_moe.astype(jnp.float32) + shared_part + routed
    return output.astype(jnp.bfloat16).reshape(1, row_count // 2, columns // 2, width_moe)


def solution(mesh):
    placed = (
        P("expert", "tile", None, None),
        P(),
        P(None, None, "tile"),
        P(None, "tile"),
        P("tile", None),
        P(),
        P(),
        P("expert", "tile"),
        P(),
        P("expert", None, None, "tile"),
        P("expert", "tile", None),
        P(None, None, "tile"),
        P("tile", None),
        P("expert", None, None, None),
        P("expert", "tile", None, None),
    )
    return jax.shard_map(
        per_device,
        mesh=mesh,
        in_specs=placed,
        out_specs=P("expert", "tile", None, None),
        check_vma=False,
    )
```

profile of v0, /device:TPU:8, one launch (start us, length us, event | category | flops | bytes accessed | tf_op | source)
XLA Modules:
  0.0 645.7 jit_solution(12023505753677855599)
XLA Ops:
  6.5 1.2 convert_reduce_fusion
  7.9 1.2 fusion.17
  9.1 1.9 fusion.20
  11.1 0.8 add.203
  11.9 0.4 multiply_cosine_fusion.1
  12.4 28.7 %all-gather.6.cloned.1.call-done = bf16[512,1152]{1,0:T(8,128)(2,1)} async-done(((bf16[128,1152]{1,0:T(8,128)(2,1)}), bf16[512,1152]{1,0:T(8,128)(2,1)}) %all-gather.6.cloned.1.call-update) | async-done | bytes 1179664 | tf_op jit(solution)/shard_map/all_gather | solution.py:115
  41.0 3.3 convolution_add_fusion
  44.4 0.1 subtract_convert_fusion.3
  44.6 1.0 subtract_convert_fusion.1
  45.6 4.5 fusion.64
  50.1 2.9 fusion.12
  53.1 1.9 convolution_convert_fusion.1
  55.0 27.5 %reduce-scatter.4.cloned.1.call-done = bf16[128,1152]{1,0:T(8,128)(2,1)} async-done(((bf16[512,1152]{1,0:T(8,128)(2,1)}), bf16[128,1152]{1,0:T(8,128)(2,1)}) %reduce-scatter.4.cloned.1.call-update) | async-done | bytes 294928 | tf_op jit(solution)/shard_map/reduce_scatter | solution.py:127
  82.5 1.1 fusion.25
  83.7 1.2 multiply_reduce_fusion.1
  84.9 1.1 multiply_convert_fusion
  86.0 0.1 reshape.328
  86.1 0.2 copy.62
  86.3 0.9 reshape.329
  87.3 0.5 all-gather.10.cloned.1.call-update
  88.0 0.1 copy.43
  88.1 0.1 copy.42
  88.3 0.1 eq.24
  88.5 2.4 reduce-window.6
  90.9 0.1 slice.153
  91.0 0.1 copy.45
  91.2 0.1 bitcast_bitcast_fusion
  91.5 36.3 %scatter_fusion = s32[4,384]{1,0:T(4,128)S(1)} fusion(s32[4,384]{1,0:T(4,128)S(1)} %broadcast_in_dim.19, s32[768]{0:T(1024)S(1)} %reshape.402, s32[768]{0:T(1024)S(1)} %reshape.404), kind=kCustom, calls=%fused_computation.7 | custom fusion | bytes 15360 | tf_op jit(solution)/shard_map/vmap()/scatter | solution.py:81
  127.8 0.1 reshape.334
  128.0 0.1 reshape.348
  128.2 67.1 %all-gather.10.cloned.1.call-done = bf16[4608,512]{1,0:T(8,128)(2,1)} async-done(((bf16[72,512]{1,0:T(8,128)(2,1)}), bf16[4608,512]{1,0:T(8,128)(2,1)}) %all-gather.10.cloned.1.call-update) | async-done | bytes 4718608 | tf_op jit(solution)/shard_map/all_gather | solution.py:144
  195.3 4.1 convolution_convert_fusion.3
  199.5 4.2 all-to-all-start
  203.7 6.0 all-to-all-done
  209.7 0.1 fusion.28
  210.0 3.1 gather_fusion
  213.1 3.7 reshape.347
  216.8 1.8 broadcast_select_fusion
  218.7 57.5 %all_to_all.23 = bf16[64,6,2048]{2,1,0:T(8,128)(2,1)S(1)} all-to-all(bf16[64,6,2048]{2,1,0:T(8,128)(2,1)S(1)} %broadcast_select_fusion), channel_id=1, replica_groups=mesh['tile'=4,'expert'=64] {'expert'}, dimensions={0} | all-to-all | bytes 3145728 | tf_op jit(solution)/shard_map/all_to_all | solution.py:173
  276.2 2.0 copy.48
  278.3 64.9 %all-gather.12.cloned.1.call-done = bf16[64,24,2048]{2,0,1:T(8,128)(2,1)} async-done(((bf16[64,6,2048]{2,0,1:T(8,128)(2,1)}), bf16[64,24,2048]{2,0,1:T(8,128)(2,1)}) %all-gather.12.cloned.1.call-update) | async-done | bytes 6291472 | tf_op jit(solution)/shard_map/all_gather | solution.py:174
  343.2 6.2 copy.49
  349.5 4.7 fusion.4
  354.1 5.6 convolution_convert_fusion
  359.7 11.1 %reshape.338 = bf16[64,4,6,2048]{3,2,1,0:T(8,128)(2,1)} reshape(bf16[1536,2048]{1,0:T(8,128)(2,1)} %convolution_convert_fusion) | data formatting | bytes 12582912 | tf_op jit(solution)/shard_map/reshape | solution.py:187
  370.8 18.9 %copy.50 = bf16[64,4,6,2048]{3,1,2,0:T(4,128)(2,1)} copy(bf16[64,4,6,2048]{3,2,1,0:T(8,128)(2,1)} %reshape.338) | data formatting | bytes 12582912 | tf_op jit(solution)/shard_map/reshape | solution.py:187
  389.7 149.8 %all_to_all.24 = bf16[64,4,6,2048]{3,1,2,0:T(4,128)(2,1)S(1)} all-to-all(bf16[64,4,6,2048]{3,1,2,0:T(4,128)(2,1)} %copy.50), channel_id=1, replica_groups=mesh['tile'=4,'expert'=64] {'expert'}, dimensions={0} | all-to-all | bytes 12582912 | tf_op jit(solution)/shard_map/all_to_all | solution.py:189
  539.4 6.1 copy.51
  545.6 14.7 %all_gather.18 = bf16[128,2048]{1,0:T(8,128)(2,1)S(1)} all-gather(bf16[32,2048]{1,0:T(8,128)(2,1)S(1)} %multiply_convert_fusion.1), channel_id=1, replica_groups=mesh['tile'=4,'expert'=64] {'tile'}, dimensions={0}, use_global_device_ids=true | all-gather | bytes 655360 | tf_op jit(solution)/shard_map/all_gather | solution.py:150
  560.3 0.9 fusion.6
  561.3 1.3 convolution_convert_fusion.2
  562.8 0.3 fusion.35
  563.1 0.6 slice_bitcast_fusion.9
  563.7 47.5 %reduce-scatter.8.cloned.1.call-done = bf16[64,1,6,2048]{3,0,2,1:T(8,128)(2,1)} async-done(((bf16[64,4,6,2048]{3,0,2,1:T(8,128)(2,1)}), bf16[64,1,6,2048]{3,0,2,1:T(8,128)(2,1)}) %reduce-scatter.8.cloned.1.call-update) | async-done | bytes 1572880 | tf_op jit(solution)/shard_map/reduce_scatter | solution.py:190
  611.2 3.6 copy.52
  614.8 2.6 reshape.339
  617.4 0.7 gather_fusion.6
  618.1 0.7 gather_fusion.5
  618.8 0.7 gather_fusion.4
  619.4 3.2 gather_fusion.3
  622.6 3.1 gather_fusion.2
  625.7 3.0 gather_fusion.1
  628.7 7.9 %reduce-scatter.6.cloned.1.call-done = bf16[32,2048]{1,0:T(8,128)(2,1)} async-done(((bf16[128,2048]{1,0:T(8,128)(2,1)}), bf16[32,2048]{1,0:T(8,128)(2,1)}) %reduce-scatter.6.cloned.1.call-update) | async-done | bytes 131088 | tf_op jit(solution)/shard_map/reduce_scatter | solution.py:155
  636.6 2.0 add_convert_fusion
  (78 shorter events, 1.5 us)
Async XLA Ops:
  6.5 342.9 %copy-start = (bf16[1,2048,2,352]{1,3,2,0:T(8,128)(2,1)S(1)}, bf16[1,2048,2,352]{1,3,2,0:T(8,128)(2,1)}, u32[]{:S(2)}) copy-start(bf16[1,2048,2,352]{1,3,2,0:T(8,128)(2,1)} %param.24) | copy-start | bytes 8650756
  6.5 34.5 %all-gather.6.cloned.1.call-start = ((), (), s32[]{:S(2)}) async-start(), calls=%async_computation.6 | async-start | bytes 1474560 | tf_op jit(solution)/shard_map/all_gather | solution.py:115
  11.1 71.4 %reduce-scatter.4.cloned.1.call-start = ((), (), s32[]{:S(2)}) async-start(), calls=%async_computation.7 | async-start | bytes 1474560 | tf_op jit(solution)/shard_map/reduce_scatter | solution.py:127
  44.3 1.3 copy-start.6
  50.1 3.0 copy-start.13
  53.0 29.5 %copy-start.3 = (bf16[1,4,32,1152]{3,2,1,0:T(8,128)(2,1)S(1)}, bf16[1,4,32,1152]{3,2,1,0:T(8,128)(2,1)}, u32[]{:S(2)}) copy-start(bf16[1,4,32,1152]{3,2,1,0:T(8,128)(2,1)} %param.15) | copy-start | bytes 884740
  53.0 29.5 %copy-start.8 = (f32[1152]{0:T(1024)S(1)}, f32[1152]{0:T(1024)}, u32[]{:S(2)}) copy-start(f32[1152]{0:T(1024)} %param.20) | copy-start | bytes 13828
  53.1 31.8 %copy-start.9 = (f32[1152]{0:T(1024)S(1)}, f32[1152]{0:T(1024)}, u32[]{:S(2)}) copy-start(f32[1152]{0:T(1024)} %param.21) | copy-start | bytes 13828
  55.0 33.0 %copy-start.7 = (s32[1,8,16,6]{2,1,3,0:T(8,128)S(1)}, s32[1,8,16,6]{2,1,3,0:T(8,128)}, u32[]{:S(2)}) copy-start(s32[1,8,16,6]{2,1,3,0:T(8,128)} %param.28) | copy-start | bytes 9220
  55.0 73.2 %all-gather.8.cloned.1.call-start = ((), (), s32[]{:S(2)}) async-start(), calls=%async_computation.8 | async-start | bytes 1474560 | tf_op jit(solution)/shard_map/all_gather | solution.py:141
  87.3 108.1 %all-gather.10.cloned.1.call-start = ((), (), s32[]{:S(2)}) async-start(), calls=%async_computation.9 | async-start | bytes 4792320 | tf_op jit(solution)/shard_map/all_gather | solution.py:144
  128.2 81.8 %copy-start.10 = (f32[2048]{0:T(1024)S(1)}, f32[2048]{0:T(1024)}, u32[]{:S(2)}) copy-start(f32[2048]{0:T(1024)} %param.23) | copy-start | bytes 24580
  199.5 10.2 %all-to-all-start = ((bf16[4,32,512]{2,1,0:T(8,128)(2,1)}), bf16[4,32,512]{2,1,0:T(8,128)(2,1)S(1)}, u32[]{:S(2)}, u32[]{:S(2)}) async-start(bf16[4,32,512]{2,1,0:T(8,128)(2,1)} %bitcast.12), calls=%async_computation.1 | async-start | bytes 262144 | tf_op jit(solution)/shard_map/all_to_all | solution.py:147
  203.7 139.5 %all-gather.12.cloned.1.call-start = ((), (), s32[]{:S(2)}) async-start(), calls=%async_computation.12 | async-start | bytes 7864320 | tf_op jit(solution)/shard_map/all_gather | solution.py:174
  278.2 333.0 %reduce-scatter.8.cloned.1.call-start = ((), (), s32[]{:S(2)}) async-start(), calls=%async_computation.11 | async-start | bytes 7864320 | tf_op jit(solution)/shard_map/reduce_scatter | solution.py:190
  349.4 4.7 copy-start.12
  545.5 14.8 %copy-start.4 = (bf16[2048,2,352]{0,2,1:T(8,128)(2,1)S(1)}, bf16[2048,2,352]{0,2,1:T(8,128)(2,1)}, u32[]{:S(2)}) copy-start(bf16[2048,2,352]{0,2,1:T(8,128)(2,1)} %param.26) | copy-start | bytes 8650756
  545.6 91.0 %reduce-scatter.6.cloned.1.call-start = ((), (), s32[]{:S(2)}) async-start(), calls=%async_computation.10 | async-start | bytes 655360 | tf_op jit(solution)/shard_map/reduce_scatter | solution.py:155
  545.6 15.6 %copy-start.5 = (bf16[352,2048]{1,0:T(8,128)(2,1)S(1)}, bf16[352,2048]{1,0:T(8,128)(2,1)}, u32[]{:S(2)}) copy-start(bf16[352,2048]{1,0:T(8,128)(2,1)} %param.27) | copy-start | bytes 4325380
  561.3 1.5 copy-start.11
  617.4 1.3 copy-start.2
  619.4 19.2 %copy-start.1 = (bf16[1,2048,2,352]{1,3,2,0:T(8,128)(2,1)S(1)}, bf16[1,2048,2,352]{1,3,2,0:T(8,128)(2,1)}, u32[]{:S(2)}) copy-start(bf16[1,2048,2,352]{1,3,2,0:T(8,128)(2,1)} %param.24) | copy-start | bytes 8650756
Sparse Core Ops, SparseCore 0:
  11.2 29.7 all-gather.5
  55.1 27.3 reduce-scatter.3
  87.4 26.7 all-gather.7
  116.8 78.5 all-gather.9
  278.3 64.8 all-gather.11
  545.7 65.4 reduce-scatter.7
  613.7 22.8 reduce-scatter.5
where the time goes:
time: 655 us; the launch traced here: 646 us
  waiting for transfers between devices  250 us (38%)
  blocking collectives  222 us (34%)
  local copies, waits for them, and re-layouts  109 us (17%)
  matrix products  29.2 us (4%)
  other arithmetic  16.6 us (3%)
  between operations  14.2 us (2%)
    all_to_all x1, blocking collectives, per_device(): lax.all_to_all(partial_out, 'expert', split_axis=0, concat_axis=0, tiled=...  150 us
    all_gather x1, waiting for transfers between devices, per_device(): lax.all_gather(proj_weight, 'expert', axis=0, tiled=True)  67.1 us
    all_gather x1, waiting for transfers between devices, per_device(): arrived = lax.all_gather(received[:, None], 'tile', axis=1, tiled=True)  64.9 us
    all_to_all x1, blocking collectives, per_device(): lax.all_to_all(outgoing, 'expert', split_axis=0, concat_axis=0, tiled=True)  57.5 us
    reduce_scatter x1, waiting for transfers between devices, per_device(): lax.psum_scatter(came_back.astype(jnp.float32).astype(jnp.bfloat16), 'til...  47.5 us
    scatter x2, local copies, waits for them, and re-layouts, block_slots(): table = jnp.full((experts_count * capacity,), -1, dtype=jnp.int32).at[pic...  36.4 us
    reshape x2, local copies, waits for them, and re-layouts, per_device(): partial_out = jnp.dot(expert_hidden, expert_out.reshape(expert_hidden.sha...  30 us
    all_gather x1, waiting for transfers between devices, per_device(): piece = lax.all_gather(normed, 'tile', axis=0, tiled=True)  28.7 us
  transfers between devices with their start and end apart: 8, of which 7 were waited for; matrix products, arithmetic and copies ran while one was open for 10% of the time, Pallas kernels for 0%

commit v1 on v0

v1 whole, which is shorter than its diff:
```python
import math

import jax
import jax.numpy as jnp
from jax import lax
from jax.experimental import pallas as pl
from jax.experimental.pallas import tpu as pltpu
from jax.sharding import PartitionSpec as P

HD = 72
NX, NY, NZ, NC = 4, 4, 8, 2
GROUP = NY * NC
CAP = 6
MESH = pl.DeviceIdType.MESH

norm_eps = 1e-06
rope_base = 10000.0


def layer_norm(values, gain_vec):
    centre = values - jnp.mean(values, axis=-1, keepdims=True)
    spread = jnp.mean(centre * centre, axis=-1, keepdims=True)
    return centre * lax.rsqrt(spread + norm_eps) * gain_vec


def rms_norm(values, gain_vec):
    return (
        values * lax.rsqrt(jnp.mean(values * values, axis=-1, keepdims=True) + norm_eps) * gain_vec
    )


def rope_tables(positions, columns, head_size):
    quarter = head_size // 4
    inverse = jnp.exp(jnp.arange(quarter).astype(jnp.float32) * (-math.log(rope_base) / quarter))
    row_angle = (positions // columns).astype(jnp.float32)[:, None] * inverse[None, :]
    col_angle = (positions % columns).astype(jnp.float32)[:, None] * inverse[None, :]
    return (jnp.cos(row_angle), jnp.sin(row_angle), jnp.cos(col_angle), jnp.sin(col_angle))


def rotate(values, tables):
    cos_row, sin_row, cos_col, sin_col = tables
    quarter = values.shape[-1] // 4
    row_a = values[..., :quarter]
    row_b = values[..., quarter : 2 * quarter]
    col_a = values[..., 2 * quarter : 3 * quarter]
    col_b = values[..., 3 * quarter :]
    return jnp.concatenate(
        [
            row_a * cos_row[:, None] - row_b * sin_row[:, None],
            row_b * cos_row[:, None] + row_a * sin_row[:, None],
            col_a * cos_col[:, None] - col_b * sin_col[:, None],
            col_b * cos_col[:, None] + col_a * sin_col[:, None],
        ],
        axis=-1,
    )


def attend(query_rows, key_rows, value_rows, divisor):
    scores = (
        jnp.einsum("qhd,khd->hqk", query_rows, key_rows, preferred_element_type=jnp.float32)
        / divisor
    )
    weights = jax.nn.softmax(scores, axis=-1).astype(jnp.bfloat16)
    attended = jnp.einsum(
        "hqk,khd->qhd", weights, value_rows, preferred_element_type=jnp.float32
    ).astype(jnp.bfloat16)
    return attended.reshape(attended.shape[0], -1)


def ring_place(axis):
    if axis == "x":
        return lax.axis_index("tile"), NX, lambda place: {"tile": place}
    here = lax.axis_index("expert")
    y, z, core = here // (NZ * NC), (here // NC) % NZ, here % NC
    return z, NZ, lambda place: {"expert": (y * NZ + place) * NC + core}


def greet(device_ids):
    barrier = pltpu.get_barrier_semaphore()
    for device_id in device_ids:
        pl.semaphore_signal(barrier, inc=1, device_id=device_id, device_id_type=MESH)
    pl.semaphore_wait(barrier, len(device_ids))


def ring_chunks(rows, step):
    starts = list(range(0, rows, step))
    half = (len(starts) + 1) // 2
    return [(s, step, 1 if i < half else -1) for i, s in enumerate(starts)]


def dir_order(chunks, sign):
    ids = range(len(chunks))
    return [i for i in ids if chunks[i][2] == sign] + [i for i in ids if chunks[i][2] != sign]


def interleave(a, b):
    out = []
    for i in range(max(len(a), len(b))):
        out += a[i : i + 1] + b[i : i + 1]
    return out


def ring_gather_kernel(plan, *refs):
    count = len(plan)
    ins, outs = refs[:count], refs[count : 2 * count]
    send_sem, recv_sem, local_sem = refs[2 * count :]
    rings = {axis: ring_place(axis) for axis, _ in plan}
    greet(
        [
            device((here + sign) % size)
            for here, size, device in rings.values()
            for sign in (1, -1)
        ]
    )
    arrivals, sends, number = {}, [], 0
    longest = max(rings[axis][1] // 2 for axis, _ in plan)
    local = []
    for hop in range(1, longest + 1):
        for task, (axis, chunks) in enumerate(plan):
            here, size, device = rings[axis]
            if hop > size // 2:
                continue
            order = interleave(
                [(1, i) for i in dir_order(chunks, 1)], [(-1, i) for i in dir_order(chunks, -1)]
            )
            for sign, i in order:
                start, rows, far = chunks[i]
                if hop == size // 2 and far != sign:
                    continue
                block = (here - sign * (hop - 1) + size) % size
                part = pl.ds(start, rows)
                if hop == 1:
                    source = ins[task].at[part]
                else:
                    arrivals.pop((task, sign, i)).wait_recv()
                    source = outs[task].at[block, part]
                copy = pltpu.make_async_remote_copy(
                    src_ref=source,
                    dst_ref=outs[task].at[block, part],
                    send_sem=send_sem.at[number],
                    recv_sem=recv_sem.at[number],
                    device_id=device((here + sign + size) % size),
                    device_id_type=MESH,
                )
                copy.start()
                arrivals[(task, sign, i)] = copy
                sends.append(copy)
                number += 1
        if hop == 1:
            for task, (axis, _) in enumerate(plan):
                own = pltpu.make_async_copy(
                    ins[task], outs[task].at[rings[axis][0]], local_sem.at[task]
                )
                own.start()
                local.append(own)
    for copy in arrivals.values():
        copy.wait_recv()
    for copy in sends:
        copy.wait_send()
    for own in local:
        own.wait()


def copies_of(axis, chunks):
    half = (NX if axis == "x" else NZ) // 2
    return sum(half + half - 1 for _ in chunks)


def ring_gather(tasks, collective_id):
    plan = [(axis, ring_chunks(block.shape[0], step)) for axis, block, step in tasks]
    copies = sum(copies_of(*entry) for entry in plan)
    sizes = {"x": NX, "z": NZ}

    def kernel(*refs):
        ring_gather_kernel(plan, *refs)

    return pl.pallas_call(
        kernel,
        out_shape=[
            jax.ShapeDtypeStruct((sizes[axis],) + block.shape, block.dtype)
            for axis, block, _ in tasks
        ],
        in_specs=[pl.BlockSpec(memory_space=pltpu.VMEM)] * len(tasks),
        out_specs=[pl.BlockSpec(memory_space=pltpu.VMEM)] * len(tasks),
        scratch_shapes=[
            pltpu.SemaphoreType.DMA((copies,)),
            pltpu.SemaphoreType.DMA((copies,)),
            pltpu.SemaphoreType.DMA((len(tasks),)),
        ],
        compiler_params=pltpu.CompilerParams(collective_id=collective_id, has_side_effects=True),
    )(*[block for _, block, _ in tasks])


def ring_reduce_kernel(axis, plan, *refs):
    count = len(plan)
    ins, outs = refs[:count], refs[count : 2 * count]
    landed, staged = refs[2 * count : 3 * count], refs[3 * count : 4 * count]
    send_sem, recv_sem = refs[4 * count :]
    here, size, device = ring_place(axis)
    greet([device((here + sign + size) % size) for sign in (1, -1)])
    half = size // 2
    last, sends, number = {}, [], 0
    slots = [0] * count
    for step in range(half):
        for task, chunks in enumerate(plan):
            order = interleave(
                [(1, i) for i in dir_order(chunks, 1)], [(-1, i) for i in dir_order(chunks, -1)]
            )
            for sign, i in order:
                start, rows, far = chunks[i]
                length = half if far == sign else half - 1
                if step >= length:
                    continue
                part = pl.ds(start, rows)
                target = (here + sign * (length - step) + size) % size
                slot = slots[task]
                slots[task] += 1
                if step == 0:
                    source = ins[task].at[target, part]
                else:
                    copy, before = last[(task, sign, i)]
                    copy.wait_recv()
                    staged[task][slot] = (
                        ins[task][target, part].astype(jnp.float32)
                        + landed[task][before].astype(jnp.float32)
                    ).astype(staged[task].dtype)
                    source = staged[task].at[slot]
                copy = pltpu.make_async_remote_copy(
                    src_ref=source,
                    dst_ref=landed[task].at[slot],
                    send_sem=send_sem.at[number],
                    recv_sem=recv_sem.at[number],
                    device_id=device((here + sign + size) % size),
                    device_id_type=MESH,
                )
                copy.start()
                last[(task, sign, i)] = (copy, slot)
                sends.append(copy)
                number += 1
    for task, chunks in enumerate(plan):
        for i, (start, rows, _) in enumerate(chunks):
            part = pl.ds(start, rows)
            total = ins[task][here, part].astype(jnp.float32)
            for sign in (1, -1):
                if (task, sign, i) in last:
                    copy, slot = last[(task, sign, i)]
                    copy.wait_recv()
                    total = total + landed[task][slot].astype(jnp.float32)
            outs[task][part] = total.astype(outs[task].dtype)
    for copy in sends:
        copy.wait_send()


def ring_reduce(axis, tasks, collective_id):
    plan = [ring_chunks(block.shape[1], step) for block, step, _ in tasks]
    copies = [copies_of(axis, chunks) for chunks in plan]

    def kernel(*refs):
        ring_reduce_kernel(axis, plan, *refs)

    boxes = [
        pltpu.VMEM((number, step, block.shape[2]), block.dtype)
        for number, (block, step, _) in zip(copies, tasks)
    ]
    return pl.pallas_call(
        kernel,
        out_shape=[jax.ShapeDtypeStruct(block.shape[1:], kind) for block, _, kind in tasks],
        in_specs=[pl.BlockSpec(memory_space=pltpu.VMEM)] * len(tasks),
        out_specs=[pl.BlockSpec(memory_space=pltpu.VMEM)] * len(tasks),
        scratch_shapes=boxes
        + boxes
        + [pltpu.SemaphoreType.DMA((sum(copies),)), pltpu.SemaphoreType.DMA((sum(copies),))],
        compiler_params=pltpu.CompilerParams(collective_id=collective_id, has_side_effects=True),
    )(*[block for block, _, _ in tasks])


def group_exchange_kernel(in_ref, out_ref, send_sem, recv_sem, local_sem):
    here = lax.axis_index("expert")
    y, z, core = here // (NZ * NC), (here // NC) % NZ, here % NC
    me = y * NC + core

    def device(member):
        return {"expert": ((member // NC) * NZ + z) * NC + member % NC}

    peers = [(me + k) % GROUP for k in range(1, GROUP)]
    greet([device(peer) for peer in peers])
    copies = []
    for k, peer in enumerate(peers):
        copy = pltpu.make_async_remote_copy(
            src_ref=in_ref.at[peer],
            dst_ref=out_ref.at[me],
            send_sem=send_sem.at[k],
            recv_sem=recv_sem.at[k],
            device_id=device(peer),
            device_id_type=MESH,
        )
        copy.start()
        copies.append(copy)
    own = pltpu.make_async_copy(in_ref.at[me], out_ref.at[me], local_sem)
    own.start()
    for copy in copies:
        copy.wait_recv()
    for copy in copies:
        copy.wait_send()
    own.wait()


def group_exchange(blocks, collective_id):
    return pl.pallas_call(
        group_exchange_kernel,
        out_shape=jax.ShapeDtypeStruct(blocks.shape, blocks.dtype),
        in_specs=[pl.BlockSpec(memory_space=pltpu.VMEM)],
        out_specs=pl.BlockSpec(memory_space=pltpu.VMEM),
        scratch_shapes=[
            pltpu.SemaphoreType.DMA((GROUP - 1,)),
            pltpu.SemaphoreType.DMA((GROUP - 1,)),
            pltpu.SemaphoreType.DMA,
        ],
        compiler_params=pltpu.CompilerParams(collective_id=collective_id, has_side_effects=True),
    )(blocks)


def slot_tables(table, tokens, top):
    picks = table[:, :top, :tokens].transpose(1, 0, 2).reshape(top, NZ * tokens)
    gates = table[:, 8 : 8 + top, :tokens].transpose(1, 0, 2).reshape(top, NZ * tokens)
    z = (lax.axis_index("expert") // NC) % NZ
    member = jnp.arange(GROUP)
    experts = ((member // NC) * NZ + z) * NC + member % NC
    match = picks[None] == experts.astype(jnp.float32)[:, None, None]
    hit = jnp.any(match, axis=1)
    gate = jnp.sum(jnp.where(match, gates[None], 0.0), axis=1)
    column = jnp.arange(NZ * tokens)
    page = column // tokens
    earlier = (page[:, None] == page[None, :]) & (column[:, None] < column[None, :])
    rank = jnp.dot(
        hit.astype(jnp.bfloat16), earlier.astype(jnp.bfloat16), preferred_element_type=jnp.float32
    )
    slot = jnp.arange(NZ * CAP)
    here = (slot // CAP)[:, None] == page[None, :]
    ranked = rank[:, None, :] == (slot % CAP).astype(jnp.float32)[None, :, None]
    chosen = here[None] & ranked & hit[:, None, :]
    select = chosen.astype(jnp.bfloat16).reshape(GROUP * NZ * CAP, NZ * tokens)
    gated = jnp.where(chosen, gate[:, None, :], 0.0).reshape(GROUP * NZ * CAP, NZ * tokens)
    return select, gated


def per_device(
    patches,
    norm1_gain,
    qkv_weight,
    qkv_bias,
    out_weight,
    out_bias,
    norm2_gain,
    proj_weight,
    moe_gain,
    expert_in,
    expert_out,
    shared_in,
    shared_out,
    routes,
    gates,
):
    tile_id = lax.axis_index("tile")
    row_count = patches.shape[1]
    columns = patches.shape[2]
    width_vit = patches.shape[3]
    local_rows = row_count * columns
    tokens = local_rows // 4
    top = routes.shape[-1]
    project = lax.all_gather(proj_weight, "expert", axis=0, tiled=True)

    inputs = patches.reshape(local_rows, width_vit).astype(jnp.float32)
    normed = layer_norm(inputs, norm1_gain).astype(jnp.bfloat16)
    own_routes = lax.dynamic_index_in_dim(
        routes.reshape(NX, tokens, top), tile_id, 0, keepdims=False
    )
    table = jnp.zeros((16, 128), jnp.float32)
    table = table.at[:top, :tokens].set(own_routes.T.astype(jnp.float32))
    table = table.at[8 : 8 + top, :tokens].set(gates.reshape(tokens, top).T)
    piece, tables_z = ring_gather([("x", normed, 32), ("z", table, 16)], 0)
    piece = piece.reshape(NX * local_rows, width_vit)

    heads_here = qkv_weight.shape[2] // HD
    qkv_flat = qkv_weight.reshape(width_vit, -1)
    bias_rows = qkv_bias.reshape(1, 3, heads_here, HD)
    mixed = (
        jnp.dot(piece, qkv_flat, preferred_element_type=jnp.float32).reshape(
            piece.shape[0], 3, heads_here, HD
        )
        + bias_rows
    )
    tables = rope_tables(jnp.arange(piece.shape[0]), columns, HD)
    attended = attend(
        rotate(mixed[:, 0], tables).astype(jnp.bfloat16),
        rotate(mixed[:, 1], tables).astype(jnp.bfloat16),
        mixed[:, 2].astype(jnp.bfloat16),
        math.sqrt(HD),
    )
    partial_rows = (
        jnp.dot(attended, out_weight, preferred_element_type=jnp.float32)
        .astype(jnp.bfloat16)
        .reshape(NX, local_rows, width_vit)
    )
    (mixed_heads,) = ring_reduce("x", [(partial_rows, 32, jnp.float32)], 1)
    hidden = inputs + mixed_heads + out_bias
    normed_out = layer_norm(hidden, norm2_gain).astype(jnp.bfloat16)
    merged = (
        normed_out.reshape(row_count // 2, 2, columns // 2, 2, width_vit)
        .transpose(0, 2, 1, 3, 4)
        .reshape(tokens, 4 * width_vit)
    )
    (group_merged,) = ring_gather([("x", merged, 16)], 2)
    select, gated = slot_tables(tables_z, tokens, top)
    projected = jnp.dot(
        group_merged.reshape(NX * tokens, -1), project, preferred_element_type=jnp.float32
    ).astype(jnp.bfloat16)
    (pieces,) = ring_gather([("x", projected, 32)], 3)
    page_tokens = pieces.transpose(1, 0, 2).reshape(NX * tokens, -1)
    width_moe = page_tokens.shape[1]
    page_in = rms_norm(page_tokens.astype(jnp.float32), moe_gain).astype(jnp.bfloat16)
    tokens_moe = lax.dynamic_slice_in_dim(page_tokens, tile_id * tokens, tokens, 0)
    moe_in = lax.dynamic_slice_in_dim(page_in, tile_id * tokens, tokens, 0)

    shared_gated = jnp.dot(
        page_in, shared_in.reshape(width_moe, -1), preferred_element_type=jnp.float32
    ).reshape(NX * tokens, 2, -1)
    shared_hidden = (jax.nn.silu(shared_gated[:, 0]) * shared_gated[:, 1]).astype(jnp.bfloat16)
    shared_rows = (
        jnp.dot(shared_hidden, shared_out, preferred_element_type=jnp.float32)
        .astype(jnp.bfloat16)
        .reshape(NX, tokens, width_moe)
    )

    (ring_in,) = ring_gather([("z", moe_in, 16)], 4)
    outgoing = jnp.dot(
        select, ring_in.reshape(NZ * tokens, width_moe), preferred_element_type=jnp.float32
    ).astype(jnp.bfloat16)
    received = group_exchange(outgoing.reshape(GROUP, NZ * CAP, width_moe), 5)
    slots = GROUP * NZ * CAP
    (arrived,) = ring_gather([("x", received.reshape(slots, width_moe), 48)], 6)
    slot_rows = arrived.reshape(NX * slots, width_moe)
    hidden_in = jnp.dot(
        slot_rows, expert_in.reshape(width_moe, -1), preferred_element_type=jnp.float32
    ).reshape(slot_rows.shape[0], 2, -1)
    expert_hidden = (jax.nn.silu(hidden_in[:, 0]) * hidden_in[:, 1]).astype(jnp.bfloat16)
    partial_out = (
        jnp.dot(
            expert_hidden,
            expert_out.reshape(expert_hidden.shape[1], width_moe),
            preferred_element_type=jnp.float32,
        )
        .astype(jnp.bfloat16)
        .reshape(NX, slots, width_moe)
    )
    results, shared_part = ring_reduce(
        "x", [(partial_out, 48, jnp.bfloat16), (shared_rows, 16, jnp.float32)], 7
    )
    returned = group_exchange(results.reshape(GROUP, NZ * CAP, width_moe), 8).reshape(
        slots, width_moe
    )
    gated_high = lax.reduce_precision(gated, 8, 7)
    gated_low = (gated - gated_high).astype(jnp.bfloat16)
    contract = (((0,), (0,)), ((), ()))
    weighted = lax.dot_general(
        gated_high.astype(jnp.bfloat16), returned, contract, preferred_element_type=jnp.float32
    ) + lax.dot_general(gated_low, returned, contract, preferred_element_type=jnp.float32)
    (routed,) = ring_reduce(
        "z", [(weighted.astype(jnp.bfloat16).reshape(NZ, tokens, width_moe), 16, jnp.float32)], 9
    )
    output = tokens_moe.astype(jnp.float32) + shared_part + routed
    return output.astype(jnp.bfloat16).reshape(1, row_count // 2, columns // 2, width_moe)


def solution(mesh):
    placed = (
        P("expert", "tile", None, None),
        P(),
        P(None, None, "tile"),
        P(None, "tile"),
        P("tile", None),
        P(),
        P(),
        P("expert", "tile"),
        P(),
        P("expert", None, None, "tile"),
        P("expert", "tile", None),
        P(None, None, "tile"),
        P("tile", None),
        P("expert", None, None, None),
        P("expert", "tile", None, None),
    )
    return jax.shard_map(
        per_device,
        mesh=mesh,
        in_specs=placed,
        out_specs=P("expert", "tile", None, None),
        check_vma=False,
    )
```

time: 655 us -> 355 us (0.54); the launches traced: 646 us -> 353 us
  Pallas kernels: 0 us -> 266 us
  waiting for transfers between devices: 250 us -> 8.08 us
  blocking collectives: 222 us -> 0 us
  local copies, waits for them, and re-layouts: 109 us -> 9.57 us
  matrix products: 29.2 us -> 40.8 us
    pallas_call x0 -> x10, Pallas kernels: none -> 266 us  [the longest x5 126 us: ring_gather(): pl.pallas_call(kernel, out_shape=[jax.ShapeDtypeStruct((sizes[axis],) + b...]
    all_to_all x2 -> x0, blocking collectives: 207 us -> none  [the longest x1 150 us: per_device(): lax.all_to_all(partial_out, 'expert', split_axis=0, concat_axis=0, tiled=...]
    all_gather x4 -> x1, waiting for transfers between devices: 161 us -> 7.37 us  [per_device(): project = lax.all_gather(proj_weight, 'expert', axis=0, tiled=True)]
    reduce_scatter x3 -> x0, waiting for transfers between devices: 82.8 us -> none  [the longest x1 47.5 us: per_device(): lax.psum_scatter(came_back.astype(jnp.float32).astype(jnp.bfloat16), 'til...]
    scatter x2, local copies, waits for them, and re-layouts: 36.4 us -> 0.4 us  [the longest x1 0.39 us: per_device(): table = table.at[8:8 + top, :tokens].set(gates.reshape(tokens, top).T)]
    reshape x6 -> x3, local copies, waits for them, and re-layouts: 32.9 us -> 1.64 us  [the longest x1 0.81 us: per_device(): routes.reshape(NX, tokens, top)]
    gather x8 -> x0, local copies, waits for them, and re-layouts: 18.1 us -> none  [the longest x6 11.2 us: per_device(): results_flat[pick_index[:, position]].astype(jnp.float32)]
    all_gather x1 -> x0, blocking collectives: 14.7 us -> none  [per_device(): group_in = lax.all_gather(moe_in, 'tile', axis=0, tiled=True)]
  transfers between devices with their start and end apart: 8 -> 1, of which waited for: 7 -> 1; matrix products, arithmetic and copies ran while one was open for 10% -> 8% of each run, Pallas kernels for 0% -> 14%
where the time goes in v1:
time: 355 us; the launch traced here: 353 us
  Pallas kernels  266 us (75%)
  matrix products  40.8 us (11%)
  other arithmetic  14.8 us (4%)
  between operations  13.9 us (4%)
  local copies, waits for them, and re-layouts  9.57 us (3%)
  waiting for transfers between devices  8.08 us (2%)
    pallas_call x5, Pallas kernels, ring_gather(): pl.pallas_call(kernel, out_shape=[jax.ShapeDtypeStruct((sizes[axis],) + b...  126 us
    pallas_call x3, Pallas kernels, ring_reduce(): pl.pallas_call(kernel, out_shape=[jax.ShapeDtypeStruct(block.shape[1:], k...  95.8 us
    pallas_call x2, Pallas kernels, group_exchange(): pl.pallas_call(group_exchange_kernel, out_shape=jax.ShapeDtypeStruct(bloc...  44.6 us
    all_gather x1, waiting for transfers between devices, per_device(): project = lax.all_gather(proj_weight, 'expert', axis=0, tiled=True)  7.37 us
  transfers between devices with their start and end apart: 1, of which 1 were waited for; matrix products, arithmetic and copies ran while one was open for 8% of the time, Pallas kernels for 14%

profile of v1, /device:TPU:8, one launch (start us, length us, event | category | flops | bytes accessed | tf_op | source)
XLA Modules:
  0.0 353.0 jit_solution(13739476016037599558)
XLA Ops:
  6.5 0.7 all-gather.2.cloned.1.call-update
  7.3 1.2 convert_reduce_fusion
  8.5 0.1 div.100
  8.6 1.2 fusion.21
  9.8 0.1 rsqrt.28
  9.9 0.8 reshape.502
  10.6 0.8 add.182
  11.4 0.7 mul.442
  12.1 0.8 reshape.501
  13.0 0.4 scatter.9.refs_1_
  13.4 0.0 copy-start.12
  13.4 1.9 fusion.24.refs_0_
  15.3 23.6 %shard_map.145 = (bf16[4,128,1152]{2,1,0:T(8,128)(2,1)}, f32[8,16,128]{2,1,0:T(8,128)}) custom-call(bf16[128,1152]{1,0:T(8,128)(2,1)} %fusion.24.refs_0_, f32[16,128]{1,0:T(8,128)} %copy-done.12), custom_call_target="tpu_custom_call" | custom-call | tf_op jit(solution)/shard_map/pallas_call | solution.py:177
  38.9 0.8 slice_bitcast_fusion.4
  39.7 0.1 broadcast_in_dim.18
  39.8 0.1 eq.80
  39.9 0.4 multiply_cosine_fusion.1
  40.3 3.3 convolution_add_fusion
  43.6 0.0 copy-start.8
  43.6 0.1 slice_bitcast_fusion.1
  43.7 0.1 subtract_convert_fusion.3
  43.9 1.0 subtract_convert_fusion.1
  44.9 4.5 %fusion.77 = (f32[4,512]{1,0:T(4,128)S(1)}, f32[4,512,512]{1,2,0:T(8,128)}) fusion(bf16[512,4,18]{0,2,1:T(8,128)(2,1)} %get-tuple-element.49, bf16[512,4,18]{0,2,1:T(8,128)(2,1)} %get-tuple-element.50, bf16[512,4,18]{0,2,1:T(8,128)(2,1)S(1)} %get-tuple-element.44, bf16[512,4,18]{0,2,1:T(8,128)(2,1)S(1)} %get-tuple-element.43, ...), kind=kOutput, calls=%fused_computation.144 | convolution fusion | flops 156500480 | bytes 4792320 | tf_op jit(solution)/shard_map/sub | solution.py:63
  49.4 2.9 fusion.14
  52.3 0.0 copy-start.1
  52.3 0.0 copy-start.10
  52.3 1.9 convolution_convert_fusion.1
  54.3 12.7 %shard_map.146 = f32[128,1152]{1,0:T(8,128)} custom-call(bf16[4,128,1152]{2,1,0:T(8,128)(2,1)} %bitcast.141), custom_call_target="tpu_custom_call" | custom-call | tf_op jit(solution)/shard_map/pallas_call | solution.py:265
  67.0 1.3 fusion.45
  68.3 1.3 multiply_reduce_fusion.1
  69.6 0.2 multiply_convert_fusion
  69.8 0.1 reshape.507
  69.9 0.2 copy.45
  70.1 0.9 reshape.508.refs_0_
  71.0 12.1 %shard_map.147 = bf16[4,32,4608]{2,1,0:T(8,128)(2,1)} custom-call(bf16[32,4608]{1,0:T(8,128)(2,1)} %reshape.508.refs_0_), custom_call_target="tpu_custom_call" | custom-call | tf_op jit(solution)/shard_map/pallas_call | solution.py:177
  83.2 0.1 compare_reduce_fusion
  83.2 0.1 fusion.50
  83.3 0.2 fusion.36
  83.5 0.1 broadcast_compare_fusion
  83.6 0.1 and_and_fusion
  83.8 7.4 %all-gather.2.cloned.1.call-done = bf16[4608,512]{1,0:T(8,128)(2,1)} async-done(((bf16[72,512]{1,0:T(8,128)(2,1)}), bf16[4608,512]{1,0:T(8,128)(2,1)}) %all-gather.2.cloned.1.call-update) | async-done | bytes 4718608 | tf_op jit(solution)/shard_map/all_gather | solution.py:371
  91.1 4.1 %convolution_convert_fusion.4.refs_0_ = bf16[128,512]{1,0:T(8,128)(2,1)} fusion(bf16[128,4608]{1,0:T(8,128)(2,1)} %bitcast.136, bf16[4608,512]{1,0:T(8,128)(2,1)} %all-gather.2.cloned.1.call-done), kind=kOutput, calls=%fused_computation.26 | convolution fusion | flops 604045312 | bytes 6029312 | tf_op jit(solution)/shard_map/dot_general | solution.py:415
  95.3 12.0 %shard_map.148 = bf16[4,128,512]{2,1,0:T(8,128)(2,1)} custom-call(bf16[128,512]{1,0:T(8,128)(2,1)} %convolution_convert_fusion.4.refs_0_), custom_call_target="tpu_custom_call" | custom-call | tf_op jit(solution)/shard_map/pallas_call | solution.py:177
  107.3 1.3 fusion.17
  108.6 0.6 dynamic-slice.16
  109.2 2.0 fusion.19
  111.2 2.1 copy.32
  113.4 0.8 copy-done.7
  114.2 0.8 fusion.34.refs_0_
  115.0 18.5 %shard_map.149 = bf16[8,32,2048]{2,1,0:T(8,128)(2,1)} custom-call(bf16[32,2048]{1,0:T(8,128)(2,1)} %fusion.34.refs_0_), custom_call_target="tpu_custom_call" | custom-call | tf_op jit(solution)/shard_map/pallas_call | solution.py:177
  133.5 3.0 convolution_convert_fusion.2
  136.5 22.3 %shard_map.150 = bf16[8,48,2048]{2,1,0:T(8,128)(2,1)} custom-call(bf16[8,48,2048]{2,1,0:T(8,128)(2,1)} %bitcast.133), custom_call_target="tpu_custom_call" | custom-call | tf_op jit(solution)/shard_map/pallas_call | solution.py:309
  158.8 59.3 %shard_map.151 = bf16[4,384,2048]{2,1,0:T(8,128)(2,1)} custom-call(bf16[384,2048]{1,0:T(8,128)(2,1)} %bitcast.135), custom_call_target="tpu_custom_call" | custom-call | tf_op jit(solution)/shard_map/pallas_call | solution.py:177
  218.1 0.0 copy-start.6
  218.1 2.8 fusion.4
  221.0 1.3 convolution_convert_fusion.3
  222.3 6.9 %fusion.6 = f32[1536,2,352]{0,2,1:T(8,128)S(1)} fusion(bf16[1536,2048,1]{1,0,2:T(8,128)(2,1)} %bitcast.134, bf16[1,2048,2,352]{1,3,2,0:T(8,128)(2,1)S(1)} %copy-done), kind=kOutput, calls=%fused_computation.9 | convolution fusion | flops 4429185024 | bytes 13500416 | tf_op jit(solution)/shard_map/dot_general | solution.py:443
  229.2 5.5 %convolution_convert_fusion = bf16[1536,2048]{1,0:T(8,128)(2,1)} fusion(bf16[1,352,2048]{2,1,0:T(8,128)(2,1)S(1)} %copy-done.17, f32[1536,2,352]{0,2,1:T(8,128)S(1)} %fusion.6), kind=kOutput, calls=%fused_computation.1 | convolution fusion | flops 2220982272 | bytes 12058624 | tf_op jit(solution)/shard_map/dot_general | solution.py:448
  234.7 63.9 %shard_map.152 = (bf16[384,2048]{1,0:T(8,128)(2,1)}, f32[32,2048]{1,0:T(8,128)}) custom-call(bf16[4,384,2048]{2,1,0:T(8,128)(2,1)} %bitcast.132, bf16[4,32,2048]{2,1,0:T(8,128)(2,1)} %bitcast.139), custom_call_target="tpu_custom_call" | custom-call | tf_op jit(solution)/shard_map/pallas_call | solution.py:265
  298.6 22.3 %shard_map.153 = bf16[8,48,2048]{2,1,0:T(8,128)(2,1)} custom-call(bf16[8,48,2048]{2,1,0:T(8,128)(2,1)} %bitcast.140), custom_call_target="tpu_custom_call" | custom-call | tf_op jit(solution)/shard_map/pallas_call | solution.py:309
  321.0 2.4 convolution_bitcast_fusion
  323.4 1.8 fusion.9
  325.2 19.3 %shard_map.154 = f32[32,2048]{1,0:T(8,128)} custom-call(bf16[8,32,2048]{2,1,0:T(8,128)(2,1)} %bitcast.145), custom_call_target="tpu_custom_call" | custom-call | tf_op jit(solution)/shard_map/pallas_call | solution.py:265
  344.5 1.7 fusion.32
  (49 shorter events, 0.2 us)
Async XLA Ops:
  6.5 215.8 %copy-start = (bf16[1,2048,2,352]{1,3,2,0:T(8,128)(2,1)S(1)}, bf16[1,2048,2,352]{1,3,2,0:T(8,128)(2,1)}, u32[]{:S(2)}) copy-start(bf16[1,2048,2,352]{1,3,2,0:T(8,128)(2,1)} %param.28) | copy-start | bytes 8650756
  6.5 84.6 %all-gather.2.cloned.1.call-start = ((), (), s32[]{:S(2)}) async-start(), calls=%async_computation | async-start | bytes 4792320 | tf_op jit(solution)/shard_map/all_gather | solution.py:371
  13.4 1.9 copy-start.12
  43.6 1.3 copy-start.8
  49.4 3.0 copy-start.18
  52.3 14.6 %copy-start.1 = (bf16[1,4,32,1152]{3,2,1,0:T(8,128)(2,1)S(1)}, bf16[1,4,32,1152]{3,2,1,0:T(8,128)(2,1)}, u32[]{:S(2)}) copy-start(bf16[1,4,32,1152]{3,2,1,0:T(8,128)(2,1)} %param.19) | copy-start | bytes 884740
  52.3 14.6 %copy-start.10 = (f32[1152]{0:T(1024)S(1)}, f32[1152]{0:T(1024)}, u32[]{:S(2)}) copy-start(f32[1152]{0:T(1024)} %param.24) | copy-start | bytes 13828
  54.3 15.3 %copy-start.13 = (f32[1152]{0:T(1024)S(1)}, f32[1152]{0:T(1024)}, u32[]{:S(2)}) copy-start(f32[1152]{0:T(1024)} %param.25) | copy-start | bytes 13828
  67.0 2.7 copy-start.2
  83.1 8.0 %copy-start.14 = (f32[48]{0:T(128)}, f32[48]{0:T(128)S(1)}, u32[]{:S(2)}) copy-start(f32[48]{0:T(128)S(1)} %get-tuple-element.62) | copy-start | bytes 580
  95.3 18.9 %copy-start.11 = (f32[2048]{0:T(1024)S(1)}, f32[2048]{0:T(1024)}, u32[]{:S(2)}) copy-start(f32[2048]{0:T(1024)} %param.27) | copy-start | bytes 24580
  107.3 6.0 %copy-start.3 = (bf16[4,128,512]{2,1,0:T(8,128)(2,1)S(1)}, bf16[4,128,512]{2,1,0:T(8,128)(2,1)}, u32[]{:S(2)}) copy-start(bf16[4,128,512]{2,1,0:T(8,128)(2,1)} %shard_map.148) | copy-start | bytes 1572868
  111.2 3.0 copy-start.16
  113.4 0.8 copy-start.7
  158.8 59.3 %copy-start.5 = (bf16[128,4,512]{0,2,1:T(8,128)(2,1)S(1)}, bf16[128,4,512]{0,2,1:T(8,128)(2,1)}, u32[]{:S(2)}) copy-start(bf16[128,4,512]{0,2,1:T(8,128)(2,1)} %copy.32) | copy-start | bytes 1572868
  218.1 2.9 copy-start.6
  222.3 6.9 %copy-start.17 = (bf16[1,352,2048]{2,1,0:T(8,128)(2,1)S(1)}, bf16[1,352,2048]{2,1,0:T(8,128)(2,1)}, u32[]{:S(2)}) copy-start(bf16[1,352,2048]{2,1,0:T(8,128)(2,1)} %param.29) | copy-start | bytes 4325380
  298.6 22.3 %copy-start.15 = (f32[48]{0:T(128)S(1)}, f32[48]{0:T(128)}, u32[]{:S(2)}) copy-start(f32[48]{0:T(128)} %copy-done.14) | copy-start | bytes 580
  320.9 2.4 copy-start.4
  323.4 21.1 %copy-start.9 = (f32[32,2048]{1,0:T(8,128)S(1)}, f32[32,2048]{1,0:T(8,128)}, u32[]{:S(2)}) copy-start(f32[32,2048]{1,0:T(8,128)} %get-tuple-element.35) | copy-start | bytes 786436
Sparse Core Ops, SparseCore 0:
  10.1 81.0 all-gather.1
